TPU v7x, 32 devices: a whole 2x2x4 slice. The times are simulated.
32 devices in a mesh: wide: 8 (over z, x), narrow: 4 (over y, core).
Axes of the slice: x: 2, y: 2, z: 4, core: 2. Of those that a mesh axis runs over, the one named last changes fastest.
Arguments:
- tokens: bfloat16 [16, 1024, 768], P('wide', 'narrow'), may hold values from -6 to 6
- segment_ids: int32 [16, 1024], P('wide'), may hold values from -1 to 7, as said below
- cotangent: bfloat16 [16, 1024, 768], P('wide', 'narrow'), may hold values from -6 to 6
- attn_w: float32 [4, 768, 768], P(None, 'wide', 'narrow')
- attn_m: float32 [4, 768, 768], P(None, 'wide', 'narrow')
- attn_v: float32 [4, 768, 768], P(None, 'wide', 'narrow')
- mlp_w: float32 [2, 768, 3072], P(None, 'wide', 'narrow')
- mlp_m: float32 [2, 768, 3072], P(None, 'wide', 'narrow')
- mlp_v: float32 [2, 768, 3072], P(None, 'wide', 'narrow')
- vectors: float32 [12, 768], replicated
- vec_m: float32 [12, 768], replicated
- vec_v: float32 [12, 768], replicated
Outputs:
- block_out: bfloat16 [16, 1024, 768], P('wide', 'narrow')
- block_input_gradient: float32 [16, 1024, 768], P('wide', 'narrow')
- attn_grad: float32 [4, 768, 768], P(None, 'wide', 'narrow')
- attn_new: float32 [4, 768, 768], P(None, 'wide', 'narrow')
- attn_m_new: float32 [4, 768, 768], P(None, 'wide', 'narrow')
- attn_v_new: float32 [4, 768, 768], P(None, 'wide', 'narrow')
- mlp_grad: float32 [2, 768, 3072], P(None, 'wide', 'narrow')
- mlp_new: float32 [2, 768, 3072], P(None, 'wide', 'narrow')
- mlp_m_new: float32 [2, 768, 3072], P(None, 'wide', 'narrow')
- mlp_v_new: float32 [2, 768, 3072], P(None, 'wide', 'narrow')
- vec_grad: float32 [12, 768], replicated
- vec_new: float32 [12, 768], replicated
- vec_m_new: float32 [12, 768], replicated
- vec_v_new: float32 [12, 768], replicated
Inputs may be any that keep to these rules, and one draw needn't show every extreme that they name: `segment_ids`: in each row the ids start at 0, never fall along the slots and are at most 7; the last slots of a row (at most 51) hold -1 for padding.
All inputs are finite; a program needn't handle non-finite values.
Results may differ from a plain program's by a relative error of at most 0.019.
Values may be sent and summed in bfloat16 or wider, within the bound.
No kernel may reach another device: no remote copies, remote signals or barrier semaphores. Data moves between devices by JAX's collectives and lax.ppermute only.
A program may use at most 128 MiB of HBM per device.

v0:
```python
import jax
import jax.numpy as jnp
from jax import lax
from jax.sharding import PartitionSpec as P

HEAD_DIM = 64
STEP = 10
EPS_NORM = 1e-06
MASKED_SCORE = -1e30
BETA_ONE = 0.5
BETA_TWO = 0.5
EPS_ADAM = 1e-08
RATE_MATRIX = 0.04
RATE_VECTOR = 0.3
DECAY_MATRIX = 0.05


def norm_shard_pieces(values_in, gain_vec, shift_vec):
    row_mean = jnp.mean(values_in, axis=-1, keepdims=True)
    centred = values_in - row_mean
    row_var = jnp.mean(centred * centred, axis=-1, keepdims=True)
    inv_std = lax.rsqrt(row_var + EPS_NORM)
    normed = centred * inv_std
    return (normed * gain_vec + shift_vec, normed, inv_std)


def norm_backward_pass(grad_out, normed, inv_std, gain_vec):
    scaled = grad_out * gain_vec
    return inv_std * (
        scaled
        - jnp.mean(scaled, axis=-1, keepdims=True)
        - normed * jnp.mean(scaled * normed, axis=-1, keepdims=True)
    )


def exact_gelu(values_in):
    return jax.nn.gelu(values_in, approximate=False)


def local_shard_portion(rows_in, sequence_count, start, count):
    shaped = rows_in.reshape(sequence_count, -1, rows_in.shape[-1])
    return lax.dynamic_slice_in_dim(shaped, start, count, 1)


def adamw_update(weight, first_mom, second, gradient, step_rate, decay_rate):
    first_new = BETA_ONE * first_mom + (1.0 - BETA_ONE) * gradient
    second_new = BETA_TWO * second + (1.0 - BETA_TWO) * gradient * gradient
    corrected = (
        first_new
        / (1.0 - BETA_ONE**STEP)
        / (jnp.sqrt(second_new / (1.0 - BETA_TWO**STEP)) + EPS_ADAM)
    )
    return (weight - step_rate * (corrected + decay_rate * weight), first_new, second_new)


def local(
    tokens,
    segment_ids,
    cotangent,
    attn_w,
    attn_m,
    attn_v,
    mlp_w,
    mlp_m,
    mlp_v,
    vectors,
    vec_m,
    vec_v,
):
    narrow_count = lax.axis_size("narrow")
    narrow_index = lax.axis_index("narrow")
    sequence_count, shard_length, width = tokens.shape
    seq_len = segment_ids.shape[1]
    token_count = sequence_count * seq_len
    local_cols = attn_w.shape[2]
    local_hidden = mlp_w.shape[2]
    head_local = local_cols // HEAD_DIM
    block_len = min(seq_len, 512)
    block_count = seq_len // block_len
    scale = HEAD_DIM ** (-0.5)
    shard_offset = narrow_index * shard_length
    attn_full, mlp_full = (
        lax.all_gather(attn_w.astype(jnp.bfloat16), "wide", axis=1, tiled=True),
        lax.all_gather(mlp_w.astype(jnp.bfloat16), "wide", axis=1, tiled=True),
    )
    tokens_all, cot_all = (
        lax.all_gather(tokens, "narrow", axis=1, tiled=True),
        lax.all_gather(cotangent, "narrow", axis=1, tiled=True),
    )
    input_tokens = tokens_all.reshape(token_count, width).astype(jnp.float32)
    cotangent_token_rows = cot_all.reshape(token_count, width)
    own_inputs = tokens.astype(jnp.float32)
    own_cot = cotangent.astype(jnp.float32)
    first_norm_gain = vectors[0]
    first_norm_bias = vectors[1]
    second_norm_gain = vectors[2]
    second_norm_bias = vectors[3]
    out_bias = vectors[4]
    down_bias = vectors[5]
    query_bias = lax.dynamic_slice_in_dim(vectors[6], narrow_index * local_cols, local_cols)
    value_bias = lax.dynamic_slice_in_dim(vectors[7], narrow_index * local_cols, local_cols)
    up_bias = lax.dynamic_slice_in_dim(
        vectors[8:].reshape(-1), narrow_index * local_hidden, local_hidden
    )
    normalized_input, first_standardized, first_inverse_std = norm_shard_pieces(
        input_tokens, first_norm_gain, first_norm_bias
    )
    norm_low = normalized_input.astype(jnp.bfloat16)
    projected = jnp.einsum(
        "td,cde->cte", norm_low, attn_full[:3], preferred_element_type=jnp.float32
    )
    col_bias = jnp.stack([query_bias, jnp.zeros_like(query_bias), value_bias])
    qkv_low = (projected + col_bias[:, None, :]).astype(jnp.bfloat16)
    queries = qkv_low[0].reshape(sequence_count, seq_len, head_local, HEAD_DIM)
    key_rows = qkv_low[1].reshape(sequence_count, seq_len, head_local, HEAD_DIM)
    value_rows = qkv_low[2].reshape(sequence_count, seq_len, head_local, HEAD_DIM)

    def scores_for(block_index):
        row_index = block_index // block_count
        start = block_index % block_count * block_len
        query_block = lax.dynamic_slice_in_dim(
            lax.dynamic_index_in_dim(queries, row_index, 0, False), start, block_len, 0
        )
        key_block = lax.dynamic_index_in_dim(key_rows, row_index, 0, False)
        value_block = lax.dynamic_index_in_dim(value_rows, row_index, 0, False)
        seg_row = lax.dynamic_index_in_dim(segment_ids, row_index, 0, False)
        seg_query = lax.dynamic_slice_in_dim(seg_row, start, block_len, 0)
        raw = (
            jnp.einsum("qhd,khd->hqk", query_block, key_block, preferred_element_type=jnp.float32)
            * scale
        )
        same_doc = seg_query[:, None] == seg_row[None, :]
        masked = jnp.where(same_doc[None], raw, MASKED_SCORE)
        return (masked, query_block, key_block, value_block, row_index, start)

    def attend(block_index):
        masked, query_block, key_block, value_block, row_index, start = scores_for(block_index)
        top_score = jnp.max(masked, axis=-1, keepdims=True)
        expo = jnp.exp(masked - top_score)
        total = jnp.sum(expo, axis=-1, keepdims=True)
        probs_low = (expo / total).astype(jnp.bfloat16)
        context = jnp.einsum(
            "hqk,khd->qhd", probs_low, value_block, preferred_element_type=jnp.float32
        ).astype(jnp.bfloat16)
        return (context, top_score[..., 0] + jnp.log(total[..., 0]))

    block_ids = jnp.arange(sequence_count * block_count)
    contexts, log_totals = lax.map(attend, block_ids)
    context_rows = contexts.reshape(token_count, local_cols)
    out_part = jnp.einsum(
        "tc,dc->td", context_rows, attn_full[3], preferred_element_type=jnp.float32
    )
    out_share = lax.psum_scatter(
        out_part.reshape(sequence_count, seq_len, width), "narrow", scatter_dimension=1, tiled=True
    )
    hidden_own = own_inputs + out_share + out_bias
    normed_two_own, second_standardized_local, inv_two_own = norm_shard_pieces(
        hidden_own, second_norm_gain, second_norm_bias
    )
    second_in = lax.all_gather(
        normed_two_own.astype(jnp.bfloat16), "narrow", axis=1, tiled=True
    ).reshape(token_count, width)
    pre_act = jnp.dot(second_in, mlp_full[0], preferred_element_type=jnp.float32) + up_bias
    activated = exact_gelu(pre_act).astype(jnp.bfloat16)
    down_part = jnp.einsum("tf,df->td", activated, mlp_full[1], preferred_element_type=jnp.float32)
    down_share = lax.psum_scatter(
        down_part.reshape(sequence_count, seq_len, width).astype(jnp.bfloat16),
        "narrow",
        scatter_dimension=1,
        tiled=True,
    ).astype(jnp.float32)
    block_own = hidden_own + down_share + down_bias
    block_out = block_own.astype(jnp.bfloat16)
    grad_down_w = jnp.einsum(
        "td,tf->df", cotangent_token_rows, activated, preferred_element_type=jnp.float32
    )
    grad_act = jnp.dot(cotangent_token_rows, mlp_full[1], preferred_element_type=jnp.float32)
    unused_value, gelu_pull = jax.vjp(exact_gelu, pre_act)
    grad_pre = gelu_pull(grad_act)[0].astype(jnp.bfloat16)
    grad_up_w = jnp.einsum("td,tf->df", second_in, grad_pre, preferred_element_type=jnp.float32)
    grad_up_bias = jnp.sum(grad_pre, axis=0, dtype=jnp.float32)
    norm_two_part = jnp.einsum(
        "tf,df->td", grad_pre, mlp_full[0], preferred_element_type=jnp.float32
    )
    second_norm_local = lax.psum_scatter(
        norm_two_part.reshape(sequence_count, seq_len, width),
        "narrow",
        scatter_dimension=1,
        tiled=True,
    )
    residual_local = own_cot + norm_backward_pass(
        second_norm_local, second_standardized_local, inv_two_own, second_norm_gain
    )
    resid_low = lax.all_gather(
        residual_local.astype(jnp.bfloat16), "narrow", axis=1, tiled=True
    ).reshape(token_count, width)
    grad_out_w = jnp.einsum(
        "td,tc->dc", resid_low, context_rows, preferred_element_type=jnp.float32
    )
    grad_context = jnp.dot(resid_low, attn_full[3], preferred_element_type=jnp.float32).astype(
        jnp.bfloat16
    )
    grad_context = grad_context.reshape(sequence_count, seq_len, head_local, HEAD_DIM)

    def attend_back(block_index):
        masked, query_block, key_block, value_block, row_index, start = scores_for(block_index)
        grad_block = lax.dynamic_slice_in_dim(
            lax.dynamic_index_in_dim(grad_context, row_index, 0, False), start, block_len, 0
        )
        log_block = lax.dynamic_index_in_dim(log_totals, block_index, 0, False)
        probs = jnp.exp(masked - log_block[..., None])
        probs_low = probs.astype(jnp.bfloat16)
        grad_values = jnp.einsum(
            "hqk,qhd->khd", probs_low, grad_block, preferred_element_type=jnp.float32
        )
        grad_probs = jnp.einsum(
            "qhd,khd->hqk", grad_block, value_block, preferred_element_type=jnp.float32
        )
        inner = jnp.sum(probs * grad_probs, axis=-1, keepdims=True)
        grad_scores = (probs * (grad_probs - inner)).astype(jnp.bfloat16)
        grad_query = (
            jnp.einsum("hqk,khd->qhd", grad_scores, key_block, preferred_element_type=jnp.float32)
            * scale
        )
        grad_keys = (
            jnp.einsum("hqk,qhd->khd", grad_scores, query_block, preferred_element_type=jnp.float32)
            * scale
        )
        return (grad_query, grad_keys, grad_values)

    query_parts, key_parts, value_parts = lax.map(attend_back, block_ids)
    grad_query_rows = query_parts.reshape(token_count, local_cols)
    grad_key_rows = (
        key_parts.reshape(sequence_count, block_count, seq_len, local_cols)
        .sum(axis=1)
        .reshape(token_count, local_cols)
    )
    grad_value_rows = (
        value_parts.reshape(sequence_count, block_count, seq_len, local_cols)
        .sum(axis=1)
        .reshape(token_count, local_cols)
    )
    grad_qkv = jnp.stack([grad_query_rows, grad_key_rows, grad_value_rows]).astype(jnp.bfloat16)
    grad_qkv_w = jnp.einsum("td,cte->cde", norm_low, grad_qkv, preferred_element_type=jnp.float32)
    grad_query_bias = jnp.sum(grad_qkv[0], axis=0, dtype=jnp.float32)
    grad_value_bias = jnp.sum(grad_qkv[2], axis=0, dtype=jnp.float32)
    norm_one_part = jnp.einsum(
        "cte,cde->td", grad_qkv, attn_full[:3], preferred_element_type=jnp.float32
    )
    first_norm_local = lax.psum_scatter(
        norm_one_part.reshape(sequence_count, seq_len, width).astype(jnp.bfloat16),
        "narrow",
        scatter_dimension=1,
        tiled=True,
    ).astype(jnp.float32)
    first_standardized_local = local_shard_portion(
        first_standardized, sequence_count, shard_offset, shard_length
    )
    first_inverse_std_local = local_shard_portion(
        first_inverse_std, sequence_count, shard_offset, shard_length
    )
    block_input_gradient = residual_local + norm_backward_pass(
        first_norm_local, first_standardized_local, first_inverse_std_local, first_norm_gain
    )
    fixed_rows = jnp.stack(
        [
            jnp.sum(first_norm_local * first_standardized_local, axis=(0, 1)),
            jnp.sum(first_norm_local, axis=(0, 1)),
            jnp.sum(second_norm_local * second_standardized_local, axis=(0, 1)),
            jnp.sum(second_norm_local, axis=(0, 1)),
            jnp.sum(residual_local, axis=(0, 1)),
            jnp.sum(own_cot, axis=(0, 1)),
        ]
    )
    head_rows = lax.dynamic_update_slice_in_dim(
        jnp.zeros((2, width), jnp.float32),
        jnp.stack([grad_query_bias, grad_value_bias]),
        narrow_index * local_cols,
        1,
    )
    up_rows = lax.dynamic_update_slice_in_dim(
        jnp.zeros((local_hidden * narrow_count,), jnp.float32),
        grad_up_bias,
        narrow_index * local_hidden,
        0,
    ).reshape(-1, width)
    vec_local = jnp.concatenate([fixed_rows, head_rows, up_rows], axis=0)
    vec_grad = lax.psum(vec_local, ("wide", "narrow"))
    attn_local = jnp.concatenate([grad_qkv_w, grad_out_w[None]], axis=0)
    mlp_local = jnp.stack([grad_up_w, grad_down_w])
    attn_grad, mlp_grad = (
        lax.psum_scatter(
            attn_local.astype(jnp.bfloat16), "wide", scatter_dimension=1, tiled=True
        ).astype(jnp.float32),
        lax.psum_scatter(
            mlp_local.astype(jnp.bfloat16), "wide", scatter_dimension=1, tiled=True
        ).astype(jnp.float32),
    )
    attn_new, attn_m_new, attn_v_new = adamw_update(
        attn_w, attn_m, attn_v, attn_grad, RATE_MATRIX, DECAY_MATRIX
    )
    mlp_new, mlp_m_new, mlp_v_new = adamw_update(
        mlp_w, mlp_m, mlp_v, mlp_grad, RATE_MATRIX, DECAY_MATRIX
    )
    vec_new, vec_m_new, vec_v_new = adamw_update(vectors, vec_m, vec_v, vec_grad, RATE_VECTOR, 0.0)
    return (
        block_out,
        block_input_gradient,
        attn_grad,
        attn_new,
        attn_m_new,
        attn_v_new,
        mlp_grad,
        mlp_new,
        mlp_m_new,
        mlp_v_new,
        vec_grad,
        vec_new,
        vec_m_new,
        vec_v_new,
    )


def solution(mesh):
    in_specs = (
        P("wide", "narrow", None),
        P("wide", None),
        P("wide", "narrow", None),
        P(None, "wide", "narrow"),
        P(None, "wide", "narrow"),
        P(None, "wide", "narrow"),
        P(None, "wide", "narrow"),
        P(None, "wide", "narrow"),
        P(None, "wide", "narrow"),
        P(),
        P(),
        P(),
    )
    out_specs = (
        P("wide", "narrow", None),
        P("wide", "narrow", None),
        P(None, "wide", "narrow"),
        P(None, "wide", "narrow"),
        P(None, "wide", "narrow"),
        P(None, "wide", "narrow"),
        P(None, "wide", "narrow"),
        P(None, "wide", "narrow"),
        P(None, "wide", "narrow"),
        P(None, "wide", "narrow"),
        P(),
        P(),
        P(),
        P(),
    )
    return jax.shard_map(local, mesh=mesh, in_specs=in_specs, out_specs=out_specs, check_vma=False)
```

profile of v0, /device:TPU:0, one launch (start us, length us, event | category | flops | bytes accessed | tf_op | source)
XLA Modules:
  0.0 722.1 jit_solution(8954707669613405270)
XLA Ops:
  11.9 45.8 %all-gather.9.cloned.1.call-done = bf16[4,768,192]{2,0,1:T(4,128)(2,1)} async-done(((bf16[4,96,192]{2,0,1:T(4,128)(2,1)}), bf16[4,768,192]{2,0,1:T(4,128)(2,1)}) %all-gather.9.cloned.1.call-update) | async-done | bytes 1179664 | tf_op jit(solution)/shard_map/all_gather | solution.py:83
  61.5 25.1 %all-gather.7.cloned.1.call-done = bf16[2,1024,768]{2,1,0:T(8,128)(2,1)} async-done(((bf16[2,256,768]{2,1,0:T(8,128)(2,1)}), bf16[2,1024,768]{2,1,0:T(8,128)(2,1)}) %all-gather.7.cloned.1.call-update) | async-done | bytes 3145744 | tf_op jit(solution)/shard_map/all_gather | solution.py:87
  89.5 3.8 convert_subtract_fusion
  100.1 39.2 %while.32 = (s32[]{:T(128)}, bf16[4,512,3,64]{1,3,2,0:T(8,128)(2,1)}, f32[4,3,512]{2,1,0:T(4,128)S(1)}, s32[4]{0:T(128)S(1)}, bf16[2,1024,3,64]{1,3,2,0:T(8,128)...) while((s32[]{:T(128)}, ...), condition=%wide.region_5.6_spmd, body=%wide.region_2.5_spmd.sunk | while | flops 422148640 | bytes 22229476 | solution.py:148
  107.1 2.7 fusion.152
  126.5 2.7 fusion.152
  142.8 4.8 fusion.97
  149.5 56.7 %reduce-scatter.9.cloned.1.call-done = f32[2,256,768]{2,1,0:T(8,128)} async-done(((f32[2,1024,768]{2,1,0:T(8,128)}), f32[2,256,768]{2,1,0:T(8,128)}) %reduce-scatter.9.cloned.1.call-update) | async-done | bytes 1572880 | tf_op jit(solution)/shard_map/reduce_scatter | solution.py:153
  210.3 50.6 %all-gather.13.cloned.1.call-done = bf16[2,768,768]{2,1,0:T(8,128)(2,1)} async-done(((bf16[2,96,768]{2,1,0:T(8,128)(2,1)}), bf16[2,768,768]{2,1,0:T(8,128)(2,1)}) %all-gather.13.cloned.1.call-update) | async-done | bytes 2359312 | tf_op jit(solution)/shard_map/all_gather | solution.py:84
  261.0 29.2 %all-gather.11.cloned.1.call-done = bf16[2,1024,768]{2,1,0:T(8,128)(2,1)} async-done(((bf16[2,256,768]{2,1,0:T(8,128)(2,1)}), bf16[2,1024,768]{2,1,0:T(8,128)(2,1)}) %all-gather.11.cloned.1.call-update) | async-done | bytes 3145744 | tf_op jit(solution)/shard_map/all_gather | solution.py:160
  290.1 19.0 %multiply_convert_fusion.1 = (bf16[2048,768]{1,0:T(8,128)(2,1)}, f32[2048,768]{1,0:T(8,128)}, f32[2048,768]{1,0:T(8,128)}) fusion(f32[768]{0:T(1024)S(1)} %dynamic_slice.110, bf16[2048,768]{1,0:T(8,128)(2,1)} %bitcast.256, bf16[2,768,768]{2,1,0:T(8,128)(2,1)} %all-gather.13.cloned.1.call-done), kind=kOutput, calls=%fused_computation.73 | convolution fusion | flops 2519728128 | bytes 20057088 | tf_op jit(solution)/shard_map/dot_general | solution.py:163
  309.1 11.1 %all-gather.15.cloned.1.call-done = bf16[2,1024,768]{2,1,0:T(8,128)(2,1)} async-done(((bf16[2,256,768]{2,1,0:T(8,128)(2,1)}), bf16[2,1024,768]{2,1,0:T(8,128)(2,1)}) %all-gather.15.cloned.1.call-update) | async-done | bytes 3145744 | tf_op jit(solution)/shard_map/all_gather | solution.py:88
  320.2 10.6 %convert_reduce_fusion = (f32[768]{0:T(1024)S(1)}, bf16[2048,768]{1,0:T(8,128)(2,1)S(1)}) fusion(f32[2048,768]{1,0:T(8,128)} %get-tuple-element.504, bf16[2048,768]{1,0:T(8,128)(2,1)} %bitcast.258, bf16[2,768,768]{2,1,0:T(8,128)(2,1)} %all-gather.13.cloned.1.call-done, f32[2048,768]{1,0:T(8,128)} %get-tuple-element.530, f32[768]{0:T(1024)S(1)} %dynamic_slice.110), kind=kOutput, calls=%fused_computation.71 | convolution fusion | flops 2442657024 | bytes 20060160 | tf_op jit(solution)/shard_map/dot_general | solution.py:177
  332.5 4.5 fusion.83
  337.0 6.6 convolution_convert_fusion.1
  343.9 51.6 %reduce-scatter.13.cloned.1.call-done = f32[2,256,768]{2,1,0:T(8,128)} async-done(((f32[2,1024,768]{2,1,0:T(8,128)}), f32[2,256,768]{2,1,0:T(8,128)}) %reduce-scatter.13.cloned.1.call-update) | async-done | bytes 1572880 | tf_op jit(solution)/shard_map/reduce_scatter | solution.py:185
  397.6 38.4 %reduce-scatter.11.cloned.1.call-done = bf16[2,256,768]{2,1,0:T(8,128)(2,1)} async-done(((bf16[2,1024,768]{2,1,0:T(8,128)(2,1)}), bf16[2,256,768]{2,1,0:T(8,128)(2,1)}) %reduce-scatter.11.cloned.1.call-update) | async-done | bytes 786448 | tf_op jit(solution)/shard_map/reduce_scatter | solution.py:166
  436.1 3.6 fusion.107
  442.9 5.6 fusion.79
  453.0 17.5 %all-gather.17.cloned.1.call-done = bf16[2,1024,768]{2,1,0:T(8,128)(2,1)} async-done(((bf16[2,256,768]{2,1,0:T(8,128)(2,1)}), bf16[2,1024,768]{2,1,0:T(8,128)(2,1)}) %all-gather.17.cloned.1.call-update) | async-done | bytes 3145744 | tf_op jit(solution)/shard_map/all_gather | solution.py:194
  470.5 3.1 convolution_convert_fusion
  476.4 64.6 %while.33 = (s32[]{:T(128)}, bf16[4,512,3,64]{1,3,2,0:T(8,128)(2,1)}, f32[4,1024,3,64]{1,3,2,0:T(8,128)}, f32[4,1024,3,64]{1,3,2,0:T(8,128)}, s32[4]{0:T(128)S(1...) while((s32[]{:T(128)}, ...), condition=%wide.region_15.16_spmd, body=%wide.region_13.15_spmd.sunk | while | flops 1031043584 | bytes 59572856 | solution.py:231
  482.7 2.8 fusion.164
  498.8 2.8 fusion.164
  514.9 2.8 fusion.164
  530.9 2.8 fusion.164
  565.2 6.2 bitcast_convert_fusion
  574.9 2.9 multiply_subtract_fusion
  578.4 50.8 %reduce-scatter.19.cloned.1.call-done = bf16[96,768]{1,0:T(8,128)(2,1)} async-done(((bf16[768,768]{1,0:T(8,128)(2,1)}), bf16[96,768]{1,0:T(8,128)(2,1)}) %reduce-scatter.19.cloned.1.call-update) | async-done | bytes 147472
  637.5 31.3 %reduce-scatter.15.cloned.1.call-done = bf16[2,256,768]{2,1,0:T(8,128)(2,1)} async-done(((bf16[2,1024,768]{2,1,0:T(8,128)(2,1)}), bf16[2,256,768]{2,1,0:T(8,128)(2,1)}) %reduce-scatter.15.cloned.1.call-update) | async-done | bytes 786448 | tf_op jit(solution)/shard_map/reduce_scatter | solution.py:250
  671.3 39.7 %psum.7 = f32[12,768]{1,0:T(8,128)S(1)} all-reduce(f32[12,768]{1,0:T(8,128)S(1)} %concatenate.8), channel_id=1, replica_groups=mesh['wide'=8,'narrow'=4] {'wide','narrow'}, use_global_device_ids=true, to_apply=%region_32.33 | all-reduce | flops 9216 | bytes 73728 | tf_op jit(solution)/shard_map/psum | solution.py:288
  711.8 3.0 fusion.72
  (269 shorter events, 141.5 us)
Async XLA Ops:
  7.2 50.5 %all-gather.9.cloned.1.call-start = ((), (), s32[]{:S(2)}) async-start(), calls=%async_computation.7 | async-start | bytes 1769472 | tf_op jit(solution)/shard_map/all_gather | solution.py:83
  9.2 77.4 %all-gather.7.cloned.1.call-start = ((), (), s32[]{:S(2)}) async-start(), calls=%async_computation.6 | async-start | bytes 3932160 | tf_op jit(solution)/shard_map/all_gather | solution.py:87
  9.9 196.2 %reduce-scatter.9.cloned.1.call-start = ((), (), s32[]{:S(2)}) async-start(), calls=%async_computation.8 | async-start | bytes 7864320 | tf_op jit(solution)/shard_map/reduce_scatter | solution.py:153
  11.8 82.1 %copy-start.24 = (f32[768]{0:T(1024)}, f32[768]{0:T(1024)S(1)}, u32[]{:S(2)}) copy-start(f32[768]{0:T(1024)S(1)} %get-tuple-element.520) | copy-start | bytes 9220
  57.7 2.9 copy-start.7
  61.5 33.7 %copy-start.16 = (bf16[3,768,192]{1,2,0:T(8,128)(2,1)}, bf16[3,768,192]{1,2,0:T(8,128)(2,1)S(1)}, u32[]{:S(2)}) copy-start(bf16[3,768,192]{1,2,0:T(8,128)(2,1)S(1)} %copy.93) | copy-start | bytes 2654212
  86.6 2.8 copy-start
  139.3 8.3 %copy-start.3 = (bf16[2,1024,3,64]{1,3,2,0:T(8,128)(2,1)}, bf16[2,1024,3,64]{1,3,2,0:T(8,128)(2,1)S(1)}, u32[]{:S(2)}) copy-start(bf16[2,1024,3,64]{1,3,2,0:T(8,128)(2,1)S(1)} %get-tuple-element.774) | copy-start | bytes 2359300
  141.4 6.2 copy-start.5
  147.6 113.3 %all-gather.13.cloned.1.call-start = ((), (), s32[]{:S(2)}) async-start(), calls=%async_computation.10 | async-start | bytes 2654208 | tf_op jit(solution)/shard_map/all_gather | solution.py:84
  149.4 140.7 %all-gather.11.cloned.1.call-start = ((), (), s32[]{:S(2)}) async-start(), calls=%async_computation.9 | async-start | bytes 3932160 | tf_op jit(solution)/shard_map/all_gather | solution.py:160
  209.6 110.6 %all-gather.15.cloned.1.call-start = ((), (), s32[]{:S(2)}) async-start(), calls=%async_computation.12 | async-start | bytes 3932160 | tf_op jit(solution)/shard_map/all_gather | solution.py:88
  210.2 185.3 %reduce-scatter.13.cloned.1.call-start = ((), (), s32[]{:S(2)}) async-start(), calls=%async_computation.13 | async-start | bytes 7864320 | tf_op jit(solution)/shard_map/reduce_scatter | solution.py:185
  320.2 12.3 %copy-start.30 = (bf16[2,768,768]{2,1,0:T(8,128)(2,1)S(1)}, bf16[2,768,768]{2,1,0:T(8,128)(2,1)}, u32[]{:S(2)}) copy-start(bf16[2,768,768]{2,1,0:T(8,128)(2,1)} %all-gather.13.cloned.1.call-done) | copy-start | bytes 7077892
  337.0 99.1 %reduce-scatter.11.cloned.1.call-start = ((), (), s32[]{:S(2)}) async-start(), calls=%async_computation.11 | async-start | bytes 3932160 | tf_op jit(solution)/shard_map/reduce_scatter | solution.py:166
  343.6 92.4 %copy-start.28 = (f32[768]{0:T(1024)S(1)}, f32[768]{0:T(1024)}, u32[]{:S(2)}) copy-start(f32[768]{0:T(1024)} %get-tuple-element.525) | copy-start | bytes 9220
  343.7 126.8 %all-gather.17.cloned.1.call-start = ((), (), s32[]{:S(2)}) async-start(), calls=%async_computation.14 | async-start | bytes 3932160 | tf_op jit(solution)/shard_map/all_gather | solution.py:194
  441.8 133.1 %reduce-scatter.17.cloned.1.call-start = ((), (), s32[]{:S(2)}) async-start(), calls=%async_computation.16 | async-start | bytes 2654208 | tf_op jit(solution)/shard_map/reduce_scatter | solution.py:295
  442.9 5.7 copy-start.29
  442.9 5.7 copy-start.32
  452.9 176.3 %reduce-scatter.19.cloned.1.call-start = ((), (), s32[]{:S(2)}) async-start(), calls=%async_computation.17 | async-start | bytes 1327104
  553.5 3.6 copy-start.10
  553.6 5.5 copy-start.21
  565.1 103.7 %reduce-scatter.15.cloned.1.call-start = ((), (), s32[]{:S(2)}) async-start(), calls=%async_computation.15 | async-start | bytes 3932160 | tf_op jit(solution)/shard_map/reduce_scatter | solution.py:250
  571.4 3.5 copy-start.14
  578.2 90.6 %copy-start.25 = (f32[768]{0:T(1024)S(1)}, f32[768]{0:T(1024)}, u32[]{:S(2)}) copy-start(f32[768]{0:T(1024)} %copy-done.24) | copy-start | bytes 9220
  631.4 79.6 %copy-start.23 = (f32[12,768]{1,0:T(8,128)S(1)}, f32[12,768]{1,0:T(8,128)}, u32[]{:S(2)}) copy-start(f32[12,768]{1,0:T(8,128)} %param.25) | copy-start | bytes 110596
  631.4 79.6 %copy-start.26 = (f32[12,768]{1,0:T(8,128)S(1)}, f32[12,768]{1,0:T(8,128)}, u32[]{:S(2)}) copy-start(f32[12,768]{1,0:T(8,128)} %param.26) | copy-start | bytes 110596
  631.4 79.6 %copy-start.27 = (f32[12,768]{1,0:T(8,128)S(1)}, f32[12,768]{1,0:T(8,128)}, u32[]{:S(2)}) copy-start(f32[12,768]{1,0:T(8,128)} %param.27) | copy-start | bytes 110596
  632.6 79.2 %copy-start.2 = (f32[2,256,768]{2,1,0:T(8,128)S(1)}, f32[2,256,768]{2,1,0:T(8,128)}, u32[]{:S(2)}) copy-start(f32[2,256,768]{2,1,0:T(8,128)} %copy-done.1) | copy-start | bytes 4718596
  668.8 43.0 %copy-start.12 = (bf16[2,256,768]{2,1,0:T(8,128)(2,1)S(1)}, bf16[2,256,768]{2,1,0:T(8,128)(2,1)}, u32[]{:S(2)}) copy-start(bf16[2,256,768]{2,1,0:T(8,128)(2,1)} %reduce-scatter.15.cloned.1.call-done) | copy-start | bytes 2359300
  711.1 3.7 copy-start.22
  (20 other events, 36.1 us)
Sparse Core Ops, SparseCore 0:
  10.8 46.8 all-gather.8
  59.2 27.3 all-gather.6
  147.8 58.3 reduce-scatter.8
  209.0 51.9 all-gather.12
  263.0 27.0 all-gather.10
  291.6 28.5 all-gather.14
  337.1 58.3 reduce-scatter.12
  398.0 37.9 reduce-scatter.10
  441.9 28.5 all-gather.16
  474.2 69.1 reduce-scatter.16
  565.3 63.9 reduce-scatter.18
  631.8 36.9 reduce-scatter.14
where the time goes:
time: 732 us; the launch traced here: 722 us
  waiting for transfers between devices  409 us (56%)
  matrix products  122 us (17%)
  other arithmetic  54.4 us (7%)
  local copies, waits for them, and re-layouts  53.4 us (7%)
  blocking collectives  39.7 us (5%)
  loops' own time  27.1 us (4%)
  between operations  15.4 us (2%)
    reduce_scatter x1, waiting for transfers between devices, local(): lax.psum_scatter(out_part.reshape(sequence_count, seq_len, width), 'narro...  56.7 us
    unnamed x13, waiting for transfers between devices  52.2 us
    reduce_scatter x1, waiting for transfers between devices, local(): lax.psum_scatter(norm_two_part.reshape(sequence_count, seq_len, width), '...  51.6 us
    all_gather x1, waiting for transfers between devices, local(): lax.all_gather(mlp_w.astype(jnp.bfloat16), 'wide', axis=1, tiled=True)  50.6 us
    all_gather x1, waiting for transfers between devices, local(): lax.all_gather(attn_w.astype(jnp.bfloat16), 'wide', axis=1, tiled=True)  45.8 us
    psum x1, blocking collectives, local(): vec_grad = lax.psum(vec_local, ('wide', 'narrow'))  39.7 us
    reduce_scatter x1, waiting for transfers between devices, local(): lax.psum_scatter(down_part.reshape(sequence_count, seq_len, width).astype...  38.4 us
    reduce_scatter x1, waiting for transfers between devices, local(): lax.psum_scatter(norm_one_part.reshape(sequence_count, seq_len, width).as...  31.3 us
  transfers between devices with their start and end apart: 12, of which 11 were waited for; matrix products, arithmetic and copies ran while one was open for 20% of the time, Pallas kernels for 0%

commit v1 on v0

--- a/solution.py
+++ b/solution.py
@@ -285,7 +285,7 @@
         0,
     ).reshape(-1, width)
     vec_local = jnp.concatenate([fixed_rows, head_rows, up_rows], axis=0)
-    vec_grad = lax.psum(vec_local, ("wide", "narrow"))
+    vec_grad = jnp.sum(lax.all_gather(vec_local, ("wide", "narrow")), axis=0)
     attn_local = jnp.concatenate([grad_qkv_w, grad_out_w[None]], axis=0)
     mlp_local = jnp.stack([grad_up_w, grad_down_w])
     attn_grad, mlp_grad = (

time: 732 us -> 809 us (1.11)
  waiting for transfers between devices: 409 us -> 527 us
  blocking collectives: 39.7 us -> 0 us
    reduce_scatter x1, waiting for transfers between devices: 0.01 us -> 65.9 us  [local(): lax.psum_scatter(mlp_local.astype(jnp.bfloat16), 'wide', scatter_dimensio...]
    all_gather x0 -> x1, waiting for transfers between devices: none -> 44.2 us  [local(): vec_grad = jnp.sum(lax.all_gather(vec_local, ('wide', 'narrow')), axis=0)]
    psum x1 -> x0, blocking collectives: 39.7 us -> none  [local(): vec_grad = lax.psum(vec_local, ('wide', 'narrow'))]
    reduce_scatter x1, waiting for transfers between devices: 31.3 us -> 14.4 us  [local(): lax.psum_scatter(norm_one_part.reshape(sequence_count, seq_len, width).as...]
    unnamed x13 -> x14, waiting for transfers between devices: 52.2 us -> 65.1 us
    all_gather x1, waiting for transfers between devices: 17.5 us -> 28.6 us  [local(): lax.all_gather(residual_local.astype(jnp.bfloat16), 'narrow', axis=1, til...]
    unnamed x79 -> x81, local copies, waits for them, and re-layouts: 25.9 us -> 25.5 us
  transfers between devices with their start and end apart: 12 -> 13, of which waited for: 11 -> 13; matrix products, arithmetic and copies ran while one was open for 20% -> 10% of each run, Pallas kernels for 0% -> 0%
where the time goes in v1:
time: 809 us; the launch traced here: 799 us
  waiting for transfers between devices  527 us (65%)
  matrix products  122 us (15%)
  other arithmetic  56.9 us (7%)
  local copies, waits for them, and re-layouts  50.5 us (6%)
  loops' own time  27 us (3%)
  between operations  15.1 us (2%)
    reduce_scatter x1, waiting for transfers between devices, local(): lax.psum_scatter(mlp_local.astype(jnp.bfloat16), 'wide', scatter_dimensio...  65.9 us
    unnamed x14, waiting for transfers between devices  65.1 us
    reduce_scatter x1, waiting for transfers between devices, local(): lax.psum_scatter(out_part.reshape(sequence_count, seq_len, width), 'narro...  56.7 us
    reduce_scatter x1, waiting for transfers between devices, local(): lax.psum_scatter(norm_two_part.reshape(sequence_count, seq_len, width), '...  51.6 us
    all_gather x1, waiting for transfers between devices, local(): lax.all_gather(mlp_w.astype(jnp.bfloat16), 'wide', axis=1, tiled=True)  50.6 us
    all_gather x1, waiting for transfers between devices, local(): lax.all_gather(attn_w.astype(jnp.bfloat16), 'wide', axis=1, tiled=True)  45.8 us
    all_gather x1, waiting for transfers between devices, local(): vec_grad = jnp.sum(lax.all_gather(vec_local, ('wide', 'narrow')), axis=0)  44.2 us
    reduce_scatter x1, waiting for transfers between devices, local(): lax.psum_scatter(down_part.reshape(sequence_count, seq_len, width).astype...  38.4 us
  transfers between devices with their start and end apart: 13, of which 13 were waited for; matrix products, arithmetic and copies ran while one was open for 10% of the time, Pallas kernels for 0%

profile of v1, /device:TPU:0, one launch (start us, length us, event | category | flops | bytes accessed | tf_op | source)
XLA Modules:
  0.0 799.0 jit_solution(14454966400560941774)
XLA Ops:
  11.9 45.8 %all-gather.12.cloned.1.call-done = bf16[4,768,192]{2,0,1:T(4,128)(2,1)} async-done(((bf16[4,96,192]{2,0,1:T(4,128)(2,1)}), bf16[4,768,192]{2,0,1:T(4,128)(2,1)}) %all-gather.12.cloned.1.call-update) | async-done | bytes 1179664 | tf_op jit(solution)/shard_map/all_gather | solution.py:83
  61.5 25.1 %all-gather.10.cloned.1.call-done = bf16[2,1024,768]{2,1,0:T(8,128)(2,1)} async-done(((bf16[2,256,768]{2,1,0:T(8,128)(2,1)}), bf16[2,1024,768]{2,1,0:T(8,128)(2,1)}) %all-gather.10.cloned.1.call-update) | async-done | bytes 3145744 | tf_op jit(solution)/shard_map/all_gather | solution.py:87
  89.5 3.8 convert_subtract_fusion
  100.1 39.2 %while.32 = (s32[]{:T(128)}, bf16[4,512,3,64]{1,3,2,0:T(8,128)(2,1)}, f32[4,3,512]{2,1,0:T(4,128)S(1)}, s32[4]{0:T(128)S(1)}, bf16[2,1024,3,64]{1,3,2,0:T(8,128)...) while((s32[]{:T(128)}, ...), condition=%wide.region_5.6_spmd, body=%wide.region_2.5_spmd.sunk | while | flops 422148640 | bytes 22229476 | solution.py:148
  107.1 2.7 fusion.152
  142.8 4.8 fusion.97
  149.5 56.7 %reduce-scatter.9.cloned.1.call-done = f32[2,256,768]{2,1,0:T(8,128)} async-done(((f32[2,1024,768]{2,1,0:T(8,128)}), f32[2,256,768]{2,1,0:T(8,128)}) %reduce-scatter.9.cloned.1.call-update) | async-done | bytes 1572880 | tf_op jit(solution)/shard_map/reduce_scatter | solution.py:153
  210.3 50.6 %all-gather.16.cloned.1.call-done = bf16[2,768,768]{2,1,0:T(8,128)(2,1)} async-done(((bf16[2,96,768]{2,1,0:T(8,128)(2,1)}), bf16[2,768,768]{2,1,0:T(8,128)(2,1)}) %all-gather.16.cloned.1.call-update) | async-done | bytes 2359312 | tf_op jit(solution)/shard_map/all_gather | solution.py:84
  261.0 29.2 %all-gather.14.cloned.1.call-done = bf16[2,1024,768]{2,1,0:T(8,128)(2,1)} async-done(((bf16[2,256,768]{2,1,0:T(8,128)(2,1)}), bf16[2,1024,768]{2,1,0:T(8,128)(2,1)}) %all-gather.14.cloned.1.call-update) | async-done | bytes 3145744 | tf_op jit(solution)/shard_map/all_gather | solution.py:160
  290.1 19.0 %multiply_convert_fusion.1 = (bf16[2048,768]{1,0:T(8,128)(2,1)}, f32[2048,768]{1,0:T(8,128)}, f32[2048,768]{1,0:T(8,128)}) fusion(f32[768]{0:T(1024)S(1)} %dynamic_slice.110, bf16[2048,768]{1,0:T(8,128)(2,1)} %bitcast.258, bf16[2,768,768]{2,1,0:T(8,128)(2,1)} %all-gather.16.cloned.1.call-done), kind=kOutput, calls=%fused_computation.73 | convolution fusion | flops 2519728128 | bytes 20057088 | tf_op jit(solution)/shard_map/dot_general | solution.py:163
  309.1 11.1 %all-gather.18.cloned.1.call-done = bf16[2,1024,768]{2,1,0:T(8,128)(2,1)} async-done(((bf16[2,256,768]{2,1,0:T(8,128)(2,1)}), bf16[2,1024,768]{2,1,0:T(8,128)(2,1)}) %all-gather.18.cloned.1.call-update) | async-done | bytes 3145744 | tf_op jit(solution)/shard_map/all_gather | solution.py:88
  320.2 10.6 %convert_reduce_fusion = (f32[768]{0:T(1024)S(1)}, bf16[2048,768]{1,0:T(8,128)(2,1)S(1)}) fusion(f32[2048,768]{1,0:T(8,128)} %get-tuple-element.504, bf16[2048,768]{1,0:T(8,128)(2,1)} %bitcast.260, bf16[2,768,768]{2,1,0:T(8,128)(2,1)} %all-gather.16.cloned.1.call-done, f32[2048,768]{1,0:T(8,128)} %get-tuple-element.530, f32[768]{0:T(1024)S(1)} %dynamic_slice.110), kind=kOutput, calls=%fused_computation.71 | convolution fusion | flops 2442657024 | bytes 20060160 | tf_op jit(solution)/shard_map/dot_general | solution.py:177
  332.5 4.5 fusion.83
  337.0 6.6 convolution_convert_fusion.1
  343.9 51.6 %reduce-scatter.13.cloned.1.call-done = f32[2,256,768]{2,1,0:T(8,128)} async-done(((f32[2,1024,768]{2,1,0:T(8,128)}), f32[2,256,768]{2,1,0:T(8,128)}) %reduce-scatter.13.cloned.1.call-update) | async-done | bytes 1572880 | tf_op jit(solution)/shard_map/reduce_scatter | solution.py:185
  397.6 38.4 %reduce-scatter.11.cloned.1.call-done = bf16[2,256,768]{2,1,0:T(8,128)(2,1)} async-done(((bf16[2,1024,768]{2,1,0:T(8,128)(2,1)}), bf16[2,256,768]{2,1,0:T(8,128)(2,1)}) %reduce-scatter.11.cloned.1.call-update) | async-done | bytes 786448 | tf_op jit(solution)/shard_map/reduce_scatter | solution.py:166
  436.1 3.6 fusion.107
  441.8 28.6 %all-gather.20.cloned.1.call-done = bf16[2,1024,768]{2,1,0:T(8,128)(2,1)} async-done(((bf16[2,256,768]{2,1,0:T(8,128)(2,1)}), bf16[2,1024,768]{2,1,0:T(8,128)(2,1)}) %all-gather.20.cloned.1.call-update) | async-done | bytes 3145744 | tf_op jit(solution)/shard_map/all_gather | solution.py:194
  470.5 3.1 convolution_convert_fusion
  476.4 64.6 %while.33 = (s32[]{:T(128)}, bf16[4,512,3,64]{1,3,2,0:T(8,128)(2,1)}, f32[4,1024,3,64]{1,3,2,0:T(8,128)}, f32[4,1024,3,64]{1,3,2,0:T(8,128)}, s32[4]{0:T(128)S(1...) while((s32[]{:T(128)}, ...), condition=%wide.region_15.16_spmd, body=%wide.region_13.15_spmd.sunk | while | flops 1031043584 | bytes 59572856 | solution.py:231
  482.5 2.8 fusion.164
  498.5 2.8 fusion.164
  514.6 2.8 fusion.164
  530.7 2.8 fusion.164
  550.8 4.1 bitcast_convert_fusion
  555.0 5.6 fusion.79
  565.6 2.8 fusion.92
  578.7 14.4 %reduce-scatter.15.cloned.1.call-done = bf16[2,256,768]{2,1,0:T(8,128)(2,1)} async-done(((bf16[2,1024,768]{2,1,0:T(8,128)(2,1)}), bf16[2,256,768]{2,1,0:T(8,128)(2,1)}) %reduce-scatter.15.cloned.1.call-update) | async-done | bytes 786448 | tf_op jit(solution)/shard_map/reduce_scatter | solution.py:250
  600.0 65.9 %reduce-scatter.17.cloned.1.call-done = bf16[2,96,768]{2,1,0:T(8,128)(2,1)} async-done(((bf16[2,768,768]{2,1,0:T(8,128)(2,1)}), bf16[2,96,768]{2,1,0:T(8,128)(2,1)}) %reduce-scatter.17.cloned.1.call-update) | async-done | bytes 294928 | tf_op jit(solution)/shard_map/reduce_scatter | solution.py:295
  668.6 63.7 %reduce-scatter.19.cloned.1.call-done = bf16[96,768]{1,0:T(8,128)(2,1)} async-done(((bf16[768,768]{1,0:T(8,128)(2,1)}), bf16[96,768]{1,0:T(8,128)(2,1)}) %reduce-scatter.19.cloned.1.call-update) | async-done | bytes 147472
  742.6 3.1 fusion.72
  745.6 44.2 %all-gather.22.cloned.1.call-done = f32[32,12,768]{2,1,0:T(8,128)} async-done(((f32[1,12,768]{2,1,0:T(8,128)}), f32[32,12,768]{2,1,0:T(8,128)}) %all-gather.22.cloned.1.call-update) | async-done | bytes 1179664 | tf_op jit(solution)/shard_map/all_gather | solution.py:288
  (274 shorter events, 146.1 us)
Async XLA Ops:
  7.2 50.5 %all-gather.12.cloned.1.call-start = ((), (), s32[]{:S(2)}) async-start(), calls=%async_computation.7 | async-start | bytes 1769472 | tf_op jit(solution)/shard_map/all_gather | solution.py:83
  9.2 77.4 %all-gather.10.cloned.1.call-start = ((), (), s32[]{:S(2)}) async-start(), calls=%async_computation.6 | async-start | bytes 3932160 | tf_op jit(solution)/shard_map/all_gather | solution.py:87
  9.9 196.2 %reduce-scatter.9.cloned.1.call-start = ((), (), s32[]{:S(2)}) async-start(), calls=%async_computation.8 | async-start | bytes 7864320 | tf_op jit(solution)/shard_map/reduce_scatter | solution.py:153
  11.8 82.1 %copy-start.25 = (f32[768]{0:T(1024)}, f32[768]{0:T(1024)S(1)}, u32[]{:S(2)}) copy-start(f32[768]{0:T(1024)S(1)} %get-tuple-element.520) | copy-start | bytes 9220
  61.5 33.7 %copy-start.14 = (bf16[3,768,192]{1,2,0:T(8,128)(2,1)}, bf16[3,768,192]{1,2,0:T(8,128)(2,1)S(1)}, u32[]{:S(2)}) copy-start(bf16[3,768,192]{1,2,0:T(8,128)(2,1)S(1)} %copy.93) | copy-start | bytes 2654212
  139.3 8.3 %copy-start.3 = (bf16[2,1024,3,64]{1,3,2,0:T(8,128)(2,1)}, bf16[2,1024,3,64]{1,3,2,0:T(8,128)(2,1)S(1)}, u32[]{:S(2)}) copy-start(bf16[2,1024,3,64]{1,3,2,0:T(8,128)(2,1)S(1)} %get-tuple-element.775) | copy-start | bytes 2359300
  141.4 6.2 copy-start.5
  147.6 113.3 %all-gather.16.cloned.1.call-start = ((), (), s32[]{:S(2)}) async-start(), calls=%async_computation.10 | async-start | bytes 2654208 | tf_op jit(solution)/shard_map/all_gather | solution.py:84
  149.4 140.7 %all-gather.14.cloned.1.call-start = ((), (), s32[]{:S(2)}) async-start(), calls=%async_computation.9 | async-start | bytes 3932160 | tf_op jit(solution)/shard_map/all_gather | solution.py:160
  209.6 110.6 %all-gather.18.cloned.1.call-start = ((), (), s32[]{:S(2)}) async-start(), calls=%async_computation.12 | async-start | bytes 3932160 | tf_op jit(solution)/shard_map/all_gather | solution.py:88
  210.2 185.3 %reduce-scatter.13.cloned.1.call-start = ((), (), s32[]{:S(2)}) async-start(), calls=%async_computation.13 | async-start | bytes 7864320 | tf_op jit(solution)/shard_map/reduce_scatter | solution.py:185
  320.2 12.3 %copy-start.31 = (bf16[2,768,768]{2,1,0:T(8,128)(2,1)S(1)}, bf16[2,768,768]{2,1,0:T(8,128)(2,1)}, u32[]{:S(2)}) copy-start(bf16[2,768,768]{2,1,0:T(8,128)(2,1)} %all-gather.16.cloned.1.call-done) | copy-start | bytes 7077892
  337.0 99.1 %reduce-scatter.11.cloned.1.call-start = ((), (), s32[]{:S(2)}) async-start(), calls=%async_computation.11 | async-start | bytes 3932160 | tf_op jit(solution)/shard_map/reduce_scatter | solution.py:166
  343.6 92.4 %copy-start.29 = (f32[768]{0:T(1024)S(1)}, f32[768]{0:T(1024)}, u32[]{:S(2)}) copy-start(f32[768]{0:T(1024)} %get-tuple-element.525) | copy-start | bytes 9220
  343.7 126.8 %all-gather.20.cloned.1.call-start = ((), (), s32[]{:S(2)}) async-start(), calls=%async_computation.14 | async-start | bytes 3932160 | tf_op jit(solution)/shard_map/all_gather | solution.py:194
  441.8 151.3 %reduce-scatter.15.cloned.1.call-start = ((), (), s32[]{:S(2)}) async-start(), calls=%async_computation.15 | async-start | bytes 3932160 | tf_op jit(solution)/shard_map/reduce_scatter | solution.py:250
  540.9 3.8 copy-start.18
  550.8 4.1 copy-start.21
  554.9 111.0 %reduce-scatter.17.cloned.1.call-start = ((), (), s32[]{:S(2)}) async-start(), calls=%async_computation.16 | async-start | bytes 2654208 | tf_op jit(solution)/shard_map/reduce_scatter | solution.py:295
  555.0 5.7 copy-start.30
  555.0 5.7 copy-start.33
  565.1 167.2 %reduce-scatter.19.cloned.1.call-start = ((), (), s32[]{:S(2)}) async-start(), calls=%async_computation.18 | async-start | bytes 1327104
  574.8 18.2 %copy-start.26 = (f32[768]{0:T(1024)S(1)}, f32[768]{0:T(1024)}, u32[]{:S(2)}) copy-start(f32[768]{0:T(1024)} %copy-done.25) | copy-start | bytes 9220
  577.1 19.6 %copy-start.13 = (f32[4,96,192]{2,1,0:T(8,128)S(1)}, f32[4,96,192]{2,1,0:T(8,128)}, u32[]{:S(2)}) copy-start(f32[4,96,192]{2,1,0:T(8,128)} %param.19) | copy-start | bytes 884740
  577.1 212.8 %all-gather.22.cloned.1.call-start = ((), (), s32[]{:S(2)}) async-start(), calls=%async_computation.17 | async-start | bytes 1622016 | tf_op jit(solution)/shard_map/all_gather | solution.py:288
  578.1 87.8 %copy-start.12 = (f32[2,96,768]{2,1,0:T(8,128)S(1)}, f32[2,96,768]{2,1,0:T(8,128)}, u32[]{:S(2)}) copy-start(f32[2,96,768]{2,1,0:T(8,128)} %param.22) | copy-start | bytes 1769476
  578.3 87.6 %copy-start.19 = (f32[2,96,768]{2,1,0:T(8,128)S(1)}, f32[2,96,768]{2,1,0:T(8,128)}, u32[]{:S(2)}) copy-start(f32[2,96,768]{2,1,0:T(8,128)} %param.23) | copy-start | bytes 1769476
  668.6 73.9 %copy-start.2 = (f32[2,256,768]{2,1,0:T(8,128)S(1)}, f32[2,256,768]{2,1,0:T(8,128)}, u32[]{:S(2)}) copy-start(f32[2,256,768]{2,1,0:T(8,128)} %copy-done.1) | copy-start | bytes 4718596
  668.6 73.9 %copy-start.10 = (bf16[2,256,768]{2,1,0:T(8,128)(2,1)S(1)}, bf16[2,256,768]{2,1,0:T(8,128)(2,1)}, u32[]{:S(2)}) copy-start(bf16[2,256,768]{2,1,0:T(8,128)(2,1)} %reduce-scatter.15.cloned.1.call-done) | copy-start | bytes 2359300
  742.5 48.8 %copy-start.24 = (f32[12,768]{1,0:T(8,128)S(1)}, f32[12,768]{1,0:T(8,128)}, u32[]{:S(2)}) copy-start(f32[12,768]{1,0:T(8,128)} %param.25) | copy-start | bytes 110596
  742.5 48.8 %copy-start.27 = (f32[12,768]{1,0:T(8,128)S(1)}, f32[12,768]{1,0:T(8,128)}, u32[]{:S(2)}) copy-start(f32[12,768]{1,0:T(8,128)} %param.26) | copy-start | bytes 110596
  742.5 48.8 %copy-start.28 = (f32[12,768]{1,0:T(8,128)S(1)}, f32[12,768]{1,0:T(8,128)}, u32[]{:S(2)}) copy-start(f32[12,768]{1,0:T(8,128)} %param.27) | copy-start | bytes 110596
  (22 other events, 42.8 us)
Sparse Core Ops, SparseCore 0:
  10.8 46.8 all-gather.11
  59.2 27.3 all-gather.9
  147.8 58.3 reduce-scatter.8
  209.0 51.9 all-gather.15
  263.0 27.0 all-gather.13
  291.6 28.5 all-gather.17
  337.1 58.3 reduce-scatter.12
  398.0 37.9 reduce-scatter.10
  441.9 28.5 all-gather.19
  555.1 37.9 reduce-scatter.14
  596.5 69.3 reduce-scatter.16
  669.2 63.1 reduce-scatter.18
  735.8 54.0 all-gather.21
